TPU v7x, 512 devices: a whole 4x8x8 slice. The times are simulated.
512 devices in a mesh: dp: 128 (over y, z, core), shard: 4 (over x).
Axes of the slice: x: 4, y: 8, z: 8, core: 2. Of those that a mesh axis runs over, the one named last changes fastest.
Arguments:
- acts: bfloat16 [131072, 1792], P('dp', 'shard'), may hold values from -6 to 6
- grad_out: bfloat16 [131072, 3584], P('dp', 'shard'), may hold values from -0.016479492 to 0.016479492
- projector: bfloat16 [1792, 256], P('shard'), may hold values from -6 to 6
- moment: bfloat16 [256, 3584], P(None, 'shard'), may hold values from -4 to 4
- second: bfloat16 [256, 3584], P(None, 'shard'), may hold values from 0.29882812 to 3
Outputs:
- new_projector: bfloat16 [1792, 256], P('shard')
- new_moment: bfloat16 [256, 3584], P(None, 'shard')
- new_second: bfloat16 [256, 3584], P(None, 'shard')
- weight_update: bfloat16 [1792, 3584], P('dp', 'shard')
All inputs are finite; a program needn't handle non-finite values.
Results may differ from a plain program's by a relative error of at most 0.0055.
Values may be sent and summed in bfloat16 or wider, within the bound.
A program may use at most 64 MiB of HBM per device.

v0:
```python
import jax
import jax.numpy as jnp
from jax import lax
from jax.sharding import PartitionSpec as P

D = 1792
RANK = 256


def shards(acts, grad_out, projector, moment, second):
    inv_width = 1.0 / D**0.5
    partial_value = jnp.dot(acts, projector, preferred_element_type=jnp.float32)
    summed = lax.psum(partial_value, "shard")
    proj_acts = (summed * inv_width).astype(jnp.bfloat16)
    local_grad = jnp.einsum("tr,tf->rf", proj_acts, grad_out, preferred_element_type=jnp.float32)
    proj_grad = lax.psum(local_grad, "dp")
    proj_low = proj_grad.astype(jnp.bfloat16)
    score_terms = jnp.einsum("tf,rf->tr", grad_out, proj_low, preferred_element_type=jnp.float32)
    token_scores = lax.psum(score_terms, "shard").astype(jnp.bfloat16)
    local_sub = jnp.einsum("td,tr->dr", acts, token_scores, preferred_element_type=jnp.float32)
    subspace = lax.psum(local_sub, "dp")
    gram_local = jnp.dot(
        subspace.T, subspace, precision=lax.Precision.HIGHEST, preferred_element_type=jnp.float32
    )
    gram_matrix = lax.psum(gram_local, "shard")
    mean_square = jnp.trace(gram_matrix) / (D * RANK) + 1e-06
    cubic = jnp.dot(
        subspace, gram_matrix, precision=lax.Precision.HIGHEST, preferred_element_type=jnp.float32
    )
    new_projector = (
        (1.5 * subspace - 0.5 * cubic / (mean_square * D)) / jnp.sqrt(mean_square)
    ).astype(jnp.bfloat16)
    moment_f = 0.9 * moment.astype(jnp.float32) + 0.1 * proj_grad
    second_f = 0.95 * second.astype(jnp.float32) + 0.05 * proj_grad * proj_grad
    first_fix = 1.0 - 0.9**20
    second_fix = 1.0 - 0.95**20
    direction = (moment_f / first_fix / (jnp.sqrt(second_f / second_fix) + 1e-08)).astype(
        jnp.bfloat16
    )
    row_count = D // lax.axis_size("dp")
    replica = lax.axis_index("dp")
    all_rows = lax.all_gather(projector, "shard", axis=0, tiled=True)
    own_rows = lax.dynamic_slice_in_dim(all_rows, replica * row_count, row_count, 0)
    weight_update = (
        jnp.dot(own_rows, direction, preferred_element_type=jnp.float32) / RANK**0.5
    ).astype(jnp.bfloat16)
    return (
        new_projector,
        moment_f.astype(jnp.bfloat16),
        second_f.astype(jnp.bfloat16),
        weight_update,
    )


def solution(mesh):
    in_specs = (
        P("dp", "shard"),
        P("dp", "shard"),
        P("shard", None),
        P(None, "shard"),
        P(None, "shard"),
    )
    out_specs = (P("shard", None), P(None, "shard"), P(None, "shard"), P("dp", "shard"))
    return jax.shard_map(shards, mesh=mesh, in_specs=in_specs, out_specs=out_specs, check_vma=False)
```

profile of v0, /device:TPU:8, one launch (start us, length us, event | category | flops | bytes accessed | tf_op | source)
XLA Modules:
  0.0 563.3 jit_solution(5339090869765811914)
XLA Ops:
  7.2 0.0 copy-start
  7.2 0.0 all-reduce.6.cloned.1.call-start
  7.2 2.9 fusion.22
  10.1 0.0 all-reduce.6.cloned.1.call-update
  10.1 0.0 all-reduce.8.cloned.1.call-start
  10.2 61.5 %all-reduce.6.cloned.1.call-done = f32[1024,256]{1,0:T(8,128)} async-done(((f32[1024,256]{1,0:T(8,128)}), f32[1024,256]{1,0:T(8,128)}) %all-reduce.6.cloned.1.call-update) | async-done | bytes 1048592 | tf_op jit(solution)/shard_map/psum | solution.py:13
  71.7 2.9 fusion.7
  74.6 0.0 all-reduce.8.cloned.1.call-update
  74.7 0.0 all-reduce.10.cloned.1.call-start
  74.7 15.0 %all_gather.3 = bf16[1792,256]{1,0:T(8,128)(2,1)} all-gather(bf16[448,256]{1,0:T(8,128)(2,1)S(1)} %copy-done.3), channel_id=1, replica_groups=mesh['dp'=128,'shard'=4] {'shard'}, dimensions={0}, use_global_device_ids=true | all-gather | bytes 1146880 | tf_op jit(solution)/shard_map/all_gather | solution.py:42
  89.8 183.2 %all-reduce.8.cloned.1.call-done = f32[256,896]{1,0:T(8,128)} async-done(((f32[256,896]{1,0:T(8,128)}), f32[256,896]{1,0:T(8,128)}) %all-reduce.8.cloned.1.call-update) | async-done | bytes 917520 | tf_op jit(solution)/shard_map/psum | solution.py:16
  273.0 1.9 convolution_bitcast_fusion
  274.9 33.3 %all-reduce.13 = bf16[1024,256]{0,1:T(8,128)(2,1)S(1)} all-reduce(f32[1024,256]{0,1:T(8,128)S(1)} %convolution_bitcast_fusion), channel_id=1, replica_groups=mesh['dp'=128,'shard'=4] {'shard'}, use_global_device_ids=true, to_apply=%region_2.0 | all-reduce | flops 262144 | bytes 1572864 | tf_op jit(solution)/shard_map/psum | solution.py:19
  308.2 2.5 convolution_bitcast_fusion.1
  310.7 0.0 all-reduce.10.cloned.1.call-update
  310.7 0.0 all-reduce.12.cloned.1.call-start
  310.8 2.6 fusion.4
  313.4 186.1 %all-reduce.10.cloned.1.call-done = f32[448,256]{1,0:T(8,128)} async-done(((f32[448,256]{1,0:T(8,128)}), f32[448,256]{1,0:T(8,128)}) %all-reduce.10.cloned.1.call-update) | async-done | bytes 458768 | tf_op jit(solution)/shard_map/psum | solution.py:21
  499.4 2.9 fusion.23
  502.3 0.0 all-reduce.12.cloned.1.call-update
  502.3 2.4 fusion.10
  504.8 47.5 %all-reduce.12.cloned.1.call-done = f32[256,256]{1,0:T(8,128)} async-done(((f32[256,256]{1,0:T(8,128)}), f32[256,256]{1,0:T(8,128)}) %all-reduce.12.cloned.1.call-update) | async-done | bytes 262160 | tf_op jit(solution)/shard_map/psum | solution.py:25
  552.2 1.6 select_reduce_fusion
  554.5 2.2 fusion.3
  (7 shorter events, 0.0 us)
Async XLA Ops:
  7.2 64.6 %copy-start = (bf16[1024,896]{1,0:T(8,128)(2,1)S(1)}, bf16[1024,896]{1,0:T(8,128)(2,1)}, u32[]{:S(2)}) copy-start(bf16[1024,896]{1,0:T(8,128)(2,1)} %param.6) | copy-start | bytes 5505028
  7.2 64.5 %all-reduce.6.cloned.1.call-start = ((), (), s32[]{:S(2)}) async-start(), calls=%async_computation | async-start | bytes 2097152 | tf_op jit(solution)/shard_map/psum | solution.py:13
  10.1 64.6 %copy-start.3 = (bf16[448,256]{1,0:T(8,128)(2,1)S(1)}, bf16[448,256]{1,0:T(8,128)(2,1)}, u32[]{:S(2)}) copy-start(bf16[448,256]{1,0:T(8,128)(2,1)} %param.7) | copy-start | bytes 688132
  10.1 262.9 %all-reduce.8.cloned.1.call-start = ((), (), s32[]{:S(2)}) async-start(), calls=%async_computation.1 | async-start | bytes 1835008 | tf_op jit(solution)/shard_map/psum | solution.py:16
  74.7 424.8 %all-reduce.10.cloned.1.call-start = ((), (), s32[]{:S(2)}) async-start(), calls=%async_computation.2 | async-start | bytes 917504 | tf_op jit(solution)/shard_map/psum | solution.py:21
  308.2 2.6 copy-start.1
  310.7 241.5 %all-reduce.12.cloned.1.call-start = ((), (), s32[]{:S(2)}) async-start(), calls=%async_computation.3 | async-start | bytes 524288 | tf_op jit(solution)/shard_map/psum | solution.py:25
  502.3 52.2 %copy-start.2 = (f32[448,256]{1,0:T(8,128)S(1)}, f32[448,256]{1,0:T(8,128)}, u32[]{:S(2)}) copy-start(f32[448,256]{1,0:T(8,128)} %all-reduce.10.cloned.1.call-done) | copy-start | bytes 1376260
Sparse Core Ops, SparseCore 0:
  10.3 61.3 all-reduce.5
  75.0 197.9 all-reduce.7
  310.9 188.5 all-reduce.9
  502.5 49.7 all-reduce.11
where the time goes:
time: 564 us; the launch traced here: 563 us
  waiting for transfers between devices  478 us (85%)
  blocking collectives  48.4 us (9%)
  matrix products  17.8 us (3%)
  between operations  14.5 us (3%)
    psum x1, waiting for transfers between devices, shards(): subspace = lax.psum(local_sub, 'dp')  186 us
    psum x1, waiting for transfers between devices, shards(): proj_grad = lax.psum(local_grad, 'dp')  183 us
    psum x1, waiting for transfers between devices, shards(): summed = lax.psum(partial_value, 'shard')  61.5 us
    psum x1, waiting for transfers between devices, shards(): gram_matrix = lax.psum(gram_local, 'shard')  47.5 us
    psum x1, blocking collectives, shards(): token_scores = lax.psum(score_terms, 'shard').astype(jnp.bfloat16)  33.3 us
    all_gather x1, blocking collectives, shards(): all_rows = lax.all_gather(projector, 'shard', axis=0, tiled=True)  15 us
  transfers between devices with their start and end apart: 4, of which 4 were waited for; matrix products, arithmetic and copies ran while one was open for 1% of the time, Pallas kernels for 0%

commit v1 on v0

--- a/solution.py
+++ b/solution.py
@@ -7,10 +7,19 @@
 RANK = 256
 
 
+def added_up(value, mesh_axis):
+    devices = lax.axis_size(mesh_axis)
+    summed, far = (value, 1)
+    while far < devices:
+        summed = summed + lax.ppermute(summed, mesh_axis, [(i, i ^ far) for i in range(devices)])
+        far = 2 * far
+    return summed
+
+
 def shards(acts, grad_out, projector, moment, second):
     inv_width = 1.0 / D**0.5
     partial_value = jnp.dot(acts, projector, preferred_element_type=jnp.float32)
-    summed = lax.psum(partial_value, "shard")
+    summed = added_up(partial_value, "shard")
     proj_acts = (summed * inv_width).astype(jnp.bfloat16)
     local_grad = jnp.einsum("tr,tf->rf", proj_acts, grad_out, preferred_element_type=jnp.float32)
     proj_grad = lax.psum(local_grad, "dp")

time: 564 us -> 558 us (0.989)
  waiting for transfers between devices: 478 us -> 466 us
  starting transfers between devices: 0.16 us -> 8.58 us
    psum x1 -> x0, waiting for transfers between devices: 61.5 us -> none  [shards(): summed = lax.psum(partial_value, 'shard')]
    ppermute x0 -> x2, waiting for transfers between devices: none -> 45.9 us  [added_up(): lax.ppermute(summed, mesh_axis, [(i, i ^ far) for i in range(devices)])]
    ppermute x0 -> x2, starting transfers between devices: none -> 8.46 us  [added_up(): lax.ppermute(summed, mesh_axis, [(i, i ^ far) for i in range(devices)])]
  transfers between devices with their start and end apart: 4 -> 5, of which waited for: 4 -> 5; matrix products, arithmetic and copies ran while one was open for 1% -> 1% of each run, Pallas kernels for 0% -> 0%
where the time goes in v1:
time: 558 us; the launch traced here: 557 us
  waiting for transfers between devices  466 us (84%)
  blocking collectives  48.7 us (9%)
  matrix products  15.5 us (3%)
  between operations  14.5 us (3%)
  starting transfers between devices  8.58 us (2%)
    psum x1, waiting for transfers between devices, shards(): proj_grad = lax.psum(local_grad, 'dp')  186 us
    psum x1, waiting for transfers between devices, shards(): subspace = lax.psum(local_sub, 'dp')  186 us
    psum x1, waiting for transfers between devices, shards(): gram_matrix = lax.psum(gram_local, 'shard')  47.5 us
    ppermute x2, waiting for transfers between devices, added_up(): lax.ppermute(summed, mesh_axis, [(i, i ^ far) for i in range(devices)])  45.9 us
    psum x1, blocking collectives, shards(): token_scores = lax.psum(score_terms, 'shard').astype(jnp.bfloat16)  33.3 us
    all_gather x1, blocking collectives, shards(): all_rows = lax.all_gather(projector, 'shard', axis=0, tiled=True)  15.4 us
  transfers between devices with their start and end apart: 5, of which 5 were waited for; matrix products, arithmetic and copies ran while one was open for 1% of the time, Pallas kernels for 0%

profile of v1, /device:TPU:8, one launch (start us, length us, event | category | flops | bytes accessed | tf_op | source)
XLA Modules:
  0.0 557.3 jit_solution(18296181119820250658)
XLA Ops:
  7.2 0.0 all-reduce.5.cloned.1.call-start
  7.2 1.8 fusion.22
  9.1 3.4 collective-permute-start
  12.5 23.4 %collective-permute-done = f32[1024,256]{1,0:T(8,128)S(1)} collective-permute-done((f32[1024,256]{1,0:T(8,128)S(1)}, f32[1024,256]{1,0:T(8,128)S(1)}, u32[]{:S(2)}, u32[]{:S(2)}) %collective-permute-start) | collective-permute-done | bytes 1048608 | tf_op jit(solution)/shard_map/ppermute | solution.py:14
  35.9 0.1 add.32
  36.0 5.1 collective-permute-start.1
  41.1 22.5 %collective-permute-done.1 = f32[1024,256]{1,0:T(8,128)S(1)} collective-permute-done((f32[1024,256]{1,0:T(8,128)S(1)}, f32[1024,256]{1,0:T(8,128)S(1)}, u32[]{:S(2)}, u32[]{:S(2)}) %collective-permute-start.1) | collective-permute-done | bytes 1048608 | tf_op jit(solution)/shard_map/ppermute | solution.py:14
  63.6 1.7 fusion.7
  65.2 0.0 all-reduce.5.cloned.1.call-update
  65.3 0.0 all-reduce.7.cloned.1.call-start
  65.3 15.4 %all_gather.3 = bf16[1792,256]{1,0:T(8,128)(2,1)} all-gather(bf16[448,256]{1,0:T(8,128)(2,1)S(1)} %copy-done.3), channel_id=1, replica_groups=mesh['dp'=128,'shard'=4] {'shard'}, dimensions={0}, use_global_device_ids=true | all-gather | bytes 1146880 | tf_op jit(solution)/shard_map/all_gather | solution.py:51
  80.7 186.4 %all-reduce.5.cloned.1.call-done = f32[256,896]{1,0:T(8,128)} async-done(((f32[256,896]{1,0:T(8,128)}), f32[256,896]{1,0:T(8,128)}) %all-reduce.5.cloned.1.call-update) | async-done | bytes 917520 | tf_op jit(solution)/shard_map/psum | solution.py:25
  267.1 1.9 convolution_bitcast_fusion
  269.0 33.3 %all-reduce.10 = bf16[1024,256]{0,1:T(8,128)(2,1)S(1)} all-reduce(f32[1024,256]{0,1:T(8,128)S(1)} %convolution_bitcast_fusion), channel_id=1, replica_groups=mesh['dp'=128,'shard'=4] {'shard'}, use_global_device_ids=true, to_apply=%region_1.0 | all-reduce | flops 262144 | bytes 1572864 | tf_op jit(solution)/shard_map/psum | solution.py:28
  302.3 2.5 convolution_bitcast_fusion.1
  304.8 0.0 all-reduce.9.cloned.1.call-start
  304.9 2.6 fusion.4
  307.4 186.1 %all-reduce.7.cloned.1.call-done = f32[448,256]{1,0:T(8,128)} async-done(((f32[448,256]{1,0:T(8,128)}), f32[448,256]{1,0:T(8,128)}) %all-reduce.7.cloned.1.call-update) | async-done | bytes 458768 | tf_op jit(solution)/shard_map/psum | solution.py:30
  493.5 2.9 fusion.23
  496.4 0.0 all-reduce.9.cloned.1.call-update
  496.4 2.4 fusion.10
  498.9 47.5 %all-reduce.9.cloned.1.call-done = f32[256,256]{1,0:T(8,128)} async-done(((f32[256,256]{1,0:T(8,128)}), f32[256,256]{1,0:T(8,128)}) %all-reduce.9.cloned.1.call-update) | async-done | bytes 262160 | tf_op jit(solution)/shard_map/psum | solution.py:34
  546.3 1.6 select_reduce_fusion
  548.6 2.2 fusion.3
  (9 shorter events, 0.0 us)
Async XLA Ops:
  7.2 56.4 %copy-start = (bf16[1024,896]{1,0:T(8,128)(2,1)S(1)}, bf16[1024,896]{1,0:T(8,128)(2,1)}, u32[]{:S(2)}) copy-start(bf16[1024,896]{1,0:T(8,128)(2,1)} %param.6) | copy-start | bytes 5505028
  7.2 259.9 %all-reduce.5.cloned.1.call-start = ((), (), s32[]{:S(2)}) async-start(), calls=%async_computation | async-start | bytes 1835008 | tf_op jit(solution)/shard_map/psum | solution.py:25
  9.1 26.8 %collective-permute-start = (f32[1024,256]{1,0:T(8,128)S(1)}, f32[1024,256]{1,0:T(8,128)S(1)}, u32[]{:S(2)}, u32[]{:S(2)}) collective-permute-start(f32[1024,256]{1,0:T(8,128)S(1)} %fusion.22), channel_id=1, source_target_pairs={{0,1},{1,0},{2,3},{3,2},{4,5},{5,4},{6,7},{7,6},{8,9},{9,8},{10,11... | collective-permute-start | bytes 3145736 | tf_op jit(solution)/shard_map/ppermute | solution.py:14
  36.0 29.3 %copy-start.3 = (bf16[448,256]{1,0:T(8,128)(2,1)S(1)}, bf16[448,256]{1,0:T(8,128)(2,1)}, u32[]{:S(2)}) copy-start(bf16[448,256]{1,0:T(8,128)(2,1)} %param.7) | copy-start | bytes 688132
  36.0 27.6 %collective-permute-start.1 = (f32[1024,256]{1,0:T(8,128)S(1)}, f32[1024,256]{1,0:T(8,128)S(1)}, u32[]{:S(2)}, u32[]{:S(2)}) collective-permute-start(f32[1024,256]{1,0:T(8,128)S(1)} %add.32), channel_id=1, source_target_pairs={{0,2},{1,3},{2,0},{3,1},{4,6},{5,7},{6,4},{7,5},{8,10},{9,11},{10,... | collective-permute-start | bytes 3145736 | tf_op jit(solution)/shard_map/ppermute | solution.py:14
  65.3 428.3 %all-reduce.7.cloned.1.call-start = ((), (), s32[]{:S(2)}) async-start(), calls=%async_computation.1 | async-start | bytes 917504 | tf_op jit(solution)/shard_map/psum | solution.py:30
  302.3 2.6 copy-start.1
  304.8 241.5 %all-reduce.9.cloned.1.call-start = ((), (), s32[]{:S(2)}) async-start(), calls=%async_computation.2 | async-start | bytes 524288 | tf_op jit(solution)/shard_map/psum | solution.py:34
  496.4 52.2 %copy-start.2 = (f32[448,256]{1,0:T(8,128)S(1)}, f32[448,256]{1,0:T(8,128)}, u32[]{:S(2)}) copy-start(f32[448,256]{1,0:T(8,128)} %all-reduce.7.cloned.1.call-done) | copy-start | bytes 1376260
Sparse Core Ops, SparseCore 0:
  65.4 201.6 all-reduce.4
  304.9 188.5 all-reduce.6
  496.5 49.7 all-reduce.8
